TPU v7x, 32 devices: a whole 2x2x4 slice. The times are simulated.
32 devices in a mesh: dp: 16 (over z, y, core), fsdp: 2 (over x).
Axes of the slice: x: 2, y: 2, z: 4, core: 2. Of those that a mesh axis runs over, the one named last changes fastest.
Arguments:
- inputs: bfloat16 [32, 1024, 768], P(('dp', 'fsdp')), may hold values from -6 to 6
- segments: int32 [32, 1024], P(('dp', 'fsdp')), may hold values from 0 to 7, never falling along the last dimension, each value on 1 to 512 neighbouring positions
- cotangent: bfloat16 [32, 1024, 768], P(('dp', 'fsdp')), may hold values from -6 to 6
- query_key_value_weight: bfloat16 [3, 768, 768], P(None, ('dp', 'fsdp')), may hold values from -0.21875 to 0.21875
- attention_out_weight: bfloat16 [768, 768], P(('dp', 'fsdp')), may hold values from -0.625 to 0.625
- feedforward_in_weight: bfloat16 [768, 3072], P(('dp', 'fsdp')), may hold values from -0.21875 to 0.21875
- feedforward_out_weight: bfloat16 [3072, 768], P(('dp', 'fsdp')), may hold values from -0.109375 to 0.109375
- projection_bias: float32 [4, 768], replicated, may hold values from -3 to 3
- hidden_unit_bias: float32 [3072], replicated, may hold values from -3 to 3
- norm_gain_rows: float32 [2, 768], replicated, may hold values from 0.25 to 1.75
- norm_shift_rows: float32 [2, 768], replicated, may hold values from -2 to 2
- adapter_down_factors: float32 [2, 768, 8], replicated, may hold values from -0.21875 to 0.21875
- adapter_up_factors: float32 [2, 8, 768], replicated, may hold values from -1.5 to 1.5
- down_first_moment: float32 [2, 768, 8], replicated, may hold values from -0.0038273276 to 0.0038273276
- up_first_moment: float32 [2, 8, 768], replicated, may hold values from -0.00057409913 to 0.00057409913
- down_second_moment: float32 [2, 768, 8], replicated, may hold values from 4.0690104e-08 to 6.5104166e-07
- up_second_moment: float32 [2, 8, 768], replicated, may hold values from 8.138021e-10 to 1.3020833e-08
- optimizer_step_count: int32 [1], replicated, may hold values from 1 to 20
Outputs:
- outputs: bfloat16 [32, 1024, 768], P(('dp', 'fsdp'))
- grad_inputs: float32 [32, 1024, 768], P(('dp', 'fsdp'))
- grad_norm: float32 [], replicated
- revised_down: float32 [2, 768, 8], replicated
- revised_up: float32 [2, 8, 768], replicated
- fresh_down_moment: float32 [2, 768, 8], replicated
- fresh_up_moment: float32 [2, 8, 768], replicated
- fresh_down_square: float32 [2, 768, 8], replicated
- fresh_up_square: float32 [2, 8, 768], replicated
Inputs may be any that keep to these rules, and one draw needn't show every extreme that they name: `segments`: ids never fall along a pack; each segment holds 1 to 512 tokens, and some segment of each draw exactly that many.
All inputs are finite; a program needn't handle non-finite values.
Results may differ from a plain program's by a relative error of at most 0.013.
The roundings to bfloat16 on the way count: a program that leaves them out, or rounds other values in their place, can miss the bound.
Values may be sent and summed in bfloat16 or wider, within the bound.
No kernel may reach another device: no remote copies, remote signals or barrier semaphores. Data moves between devices by JAX's collectives and lax.ppermute only.
A program may use at most 256 MiB of HBM per device.

v0:
```python
import jax
import jax.numpy as jnp
from jax import lax
from jax.sharding import PartitionSpec as P

HEAD_DIM = 64


ln_eps = 1e-05
adapter_alpha = 16.0
clip_max = 1.0
beta_one = 0.9
beta_two = 0.999
adam_eps = 1e-08
down_learning_rate = 0.02
up_learning_rate = 0.32
down_decay_factor = 0.1
up_decay_factor = 0.01
mask_fill = -1000000000.0
block_rows = 512


def matmul(left, right):
    return jnp.dot(left, right, preferred_element_type=jnp.float32)


def layer_norm(pre_values, gain_row, shift_row):
    average = jnp.mean(pre_values, axis=-1, keepdims=True)
    centered = pre_values - average
    variance = jnp.mean(centered * centered, axis=-1, keepdims=True)
    return centered * lax.rsqrt(variance + ln_eps) * gain_row + shift_row


def gelu_exact(pre_values):
    return jax.nn.gelu(pre_values, approximate=False)


def adamw_update(
    weight_old, gradient, first_old, second_old, finished_steps, step_rate, decay_rate
):
    first_new = beta_one * first_old + (1.0 - beta_one) * gradient
    second_new = beta_two * second_old + (1.0 - beta_two) * gradient * gradient
    first_hat = first_new / (1.0 - jnp.power(beta_one, finished_steps))
    second_hat = second_new / (1.0 - jnp.power(beta_two, finished_steps))
    weight_new = weight_old - step_rate * (
        first_hat / (jnp.sqrt(second_hat) + adam_eps) + decay_rate * weight_old
    )
    return (weight_new, first_new, second_new)


def attention_forward(queries, key_rows, values, segment, head_dim):
    length, model_width = queries.shape
    head_count = model_width // head_dim
    block_size = min(block_rows, length)
    score_scale = float(head_dim) ** (-0.5)
    key_heads = key_rows.reshape(length, head_count, head_dim)
    value_heads = values.reshape(length, head_count, head_dim)

    def one_block(number):
        offset = number * block_size
        query_block = lax.dynamic_slice_in_dim(queries, offset, block_size, 0).reshape(
            block_size, head_count, head_dim
        )
        row_doc = lax.dynamic_slice_in_dim(segment, offset, block_size, 0)
        scores = (
            jnp.einsum("qhd,khd->hqk", query_block, key_heads, preferred_element_type=jnp.float32)
            * score_scale
        )
        masked = jnp.where((row_doc[:, None] == segment[None, :])[None], scores, mask_fill)
        row_peak = jnp.max(masked, axis=-1, keepdims=True)
        exponent = jnp.exp(masked - row_peak)
        row_total = jnp.sum(exponent, axis=-1, keepdims=True)
        soft_weights = (exponent / row_total).astype(jnp.bfloat16)
        attended = jnp.einsum(
            "hqk,khd->qhd", soft_weights, value_heads, preferred_element_type=jnp.float32
        )
        log_total = row_peak[..., 0] + jnp.log(row_total[..., 0])
        return (attended.reshape(block_size, model_width).astype(jnp.bfloat16), log_total)

    attended, log_total = lax.map(one_block, jnp.arange(length // block_size))
    return (attended.reshape(length, model_width), log_total)


def attention_backward(queries, key_rows, values, segment, log_total, grad_attended, head_dim):
    length, model_width = queries.shape
    head_count = model_width // head_dim
    block_size = min(block_rows, length)
    score_scale = float(head_dim) ** (-0.5)
    key_heads = key_rows.reshape(length, head_count, head_dim)
    value_heads = values.reshape(length, head_count, head_dim)

    def one_block(running, number):
        grad_key_sum, grad_value_sum = running
        offset = number * block_size
        query_block = lax.dynamic_slice_in_dim(queries, offset, block_size, 0).reshape(
            block_size, head_count, head_dim
        )
        grad_block = lax.dynamic_slice_in_dim(grad_attended, offset, block_size, 0).reshape(
            block_size, head_count, head_dim
        )
        row_doc = lax.dynamic_slice_in_dim(segment, offset, block_size, 0)
        row_log = log_total[number]
        scores = (
            jnp.einsum("qhd,khd->hqk", query_block, key_heads, preferred_element_type=jnp.float32)
            * score_scale
        )
        masked = jnp.where((row_doc[:, None] == segment[None, :])[None], scores, mask_fill)
        soft_weights = jnp.exp(masked - row_log[:, :, None])
        grad_soft = jnp.einsum(
            "qhd,khd->hqk", grad_block, value_heads, preferred_element_type=jnp.float32
        )
        row_inner = jnp.sum(soft_weights * grad_soft, axis=-1, keepdims=True)
        grad_scores = (soft_weights * (grad_soft - row_inner)).astype(jnp.bfloat16)
        grad_rows = (
            jnp.einsum("hqk,khd->qhd", grad_scores, key_heads, preferred_element_type=jnp.float32)
            * score_scale
        )
        grad_key_sum = (
            grad_key_sum
            + jnp.einsum(
                "hqk,qhd->khd", grad_scores, query_block, preferred_element_type=jnp.float32
            )
            * score_scale
        )
        grad_value_sum = grad_value_sum + jnp.einsum(
            "hqk,qhd->khd",
            soft_weights.astype(jnp.bfloat16),
            grad_block,
            preferred_element_type=jnp.float32,
        )
        return ((grad_key_sum, grad_value_sum), grad_rows.reshape(block_size, model_width))

    zero_heads = jnp.zeros((length, head_count, head_dim), jnp.float32)
    (grad_keys, grad_values), grad_rows = lax.scan(
        one_block, (zero_heads, zero_heads), jnp.arange(length // block_size)
    )
    return (
        grad_rows.reshape(length, model_width),
        grad_keys.reshape(length, model_width),
        grad_values.reshape(length, model_width),
    )


def forward_pack(token_rows, segment, weights, params, head_dim):
    attn_full, output_full, expand_full, reduce_full = weights
    down_reduced, up_low, projection_bias, hidden_unit_bias, norm_gain_rows, norm_shift_rows = (
        params
    )
    adapter_scale = adapter_alpha / down_reduced.shape[-1]
    adapter_rows = jnp.einsum(
        "td,gdr->gtr", token_rows, down_reduced, preferred_element_type=jnp.float32
    ).astype(jnp.bfloat16)
    projected = jnp.einsum("td,gde->gte", token_rows, attn_full, preferred_element_type=jnp.float32)
    lifted = jnp.einsum("gtr,grd->gtd", adapter_rows, up_low, preferred_element_type=jnp.float32)
    queries = (projected[0] + projection_bias[0] + adapter_scale * lifted[0]).astype(jnp.bfloat16)
    key_rows = projected[1].astype(jnp.bfloat16)
    values = (projected[2] + projection_bias[1] + adapter_scale * lifted[1]).astype(jnp.bfloat16)
    attended, log_total = attention_forward(queries, key_rows, values, segment, head_dim)
    pre_first = token_rows.astype(jnp.float32) + (
        matmul(attended, output_full) + projection_bias[2]
    )
    normed_first = layer_norm(pre_first, norm_gain_rows[0], norm_shift_rows[0])
    hidden = matmul(normed_first.astype(jnp.bfloat16), expand_full) + hidden_unit_bias
    active = gelu_exact(hidden).astype(jnp.bfloat16)
    pre_second = normed_first + (matmul(active, reduce_full) + projection_bias[3])
    final_output = layer_norm(pre_second, norm_gain_rows[1], norm_shift_rows[1]).astype(
        jnp.bfloat16
    )
    saved = (queries, key_rows, values, log_total, adapter_rows, pre_first, hidden, pre_second)
    return (final_output, saved)


def backward_pack(token_rows, segment, pack_cot, saved, weights, params, head_dim):
    attn_full, output_full, expand_full, reduce_full = weights
    down_reduced, up_low, projection_bias, hidden_unit_bias, norm_gain_rows, norm_shift_rows = (
        params
    )
    queries, key_rows, values, log_total, adapter_rows, pre_first, hidden, pre_second = saved
    adapter_scale = adapter_alpha / down_reduced.shape[-1]

    def norm_second(pre_values):
        return layer_norm(pre_values, norm_gain_rows[1], norm_shift_rows[1])

    def norm_first(pre_values):
        return layer_norm(pre_values, norm_gain_rows[0], norm_shift_rows[0])

    unused_second, second_pull = jax.vjp(norm_second, pre_second)
    grad_second = second_pull(pack_cot.astype(jnp.float32))[0]
    grad_active = matmul(grad_second.astype(jnp.bfloat16), reduce_full.T)
    unused_gelu, gelu_pull = jax.vjp(gelu_exact, hidden)
    grad_hidden = gelu_pull(grad_active)[0].astype(jnp.bfloat16)
    grad_normed = grad_second + matmul(grad_hidden, expand_full.T)
    unused_first, first_pull = jax.vjp(norm_first, pre_first)
    grad_first = first_pull(grad_normed)[0]
    grad_attended = matmul(grad_first.astype(jnp.bfloat16), output_full.T).astype(jnp.bfloat16)
    grad_queries, grad_keys, grad_values = attention_backward(
        queries, key_rows, values, segment, log_total, grad_attended, head_dim
    )
    grad_proj = jnp.stack([grad_queries, grad_keys, grad_values]).astype(jnp.bfloat16)
    adapted = jnp.stack([grad_proj[0], grad_proj[2]])
    grad_up = adapter_scale * jnp.einsum(
        "gtr,gtd->grd", adapter_rows, adapted, preferred_element_type=jnp.float32
    )
    grad_adapter = (
        adapter_scale
        * jnp.einsum("gtd,grd->gtr", adapted, up_low, preferred_element_type=jnp.float32)
    ).astype(jnp.bfloat16)
    grad_down = jnp.einsum(
        "td,gtr->gdr", token_rows, grad_adapter, preferred_element_type=jnp.float32
    )
    grad_tokens = grad_first + jnp.einsum(
        "gte,gde->td", grad_proj, attn_full, preferred_element_type=jnp.float32
    )
    grad_tokens = grad_tokens + jnp.einsum(
        "gtr,gdr->td", grad_adapter, down_reduced, preferred_element_type=jnp.float32
    )
    return (grad_tokens, grad_down, grad_up)


def shards(
    inputs,
    segments,
    cotangent,
    query_key_value_weight,
    attention_out_weight,
    feedforward_in_weight,
    feedforward_out_weight,
    projection_bias,
    hidden_unit_bias,
    norm_gain_rows,
    norm_shift_rows,
    adapter_down_factors,
    adapter_up_factors,
    down_first_moment,
    up_first_moment,
    down_second_moment,
    up_second_moment,
    optimizer_step_count,
):
    head_dim = HEAD_DIM
    weights = (
        lax.all_gather(query_key_value_weight, ("dp", "fsdp"), axis=1, tiled=True),
        lax.all_gather(attention_out_weight, ("dp", "fsdp"), axis=0, tiled=True),
        lax.all_gather(feedforward_in_weight, ("dp", "fsdp"), axis=0, tiled=True),
        lax.all_gather(feedforward_out_weight, ("dp", "fsdp"), axis=0, tiled=True),
    )
    params = (
        adapter_down_factors.astype(jnp.bfloat16),
        adapter_up_factors.astype(jnp.bfloat16),
        projection_bias,
        hidden_unit_bias,
        norm_gain_rows,
        norm_shift_rows,
    )

    def forward_step(unused, slices):
        final_output, saved = forward_pack(slices[0], slices[1], weights, params, head_dim)
        return (unused, (final_output, saved))

    unused_carry, (outputs, saved_all) = lax.scan(
        forward_step, jnp.zeros((), jnp.float32), (inputs, segments)
    )
    back_weights = (
        lax.all_gather(query_key_value_weight, ("dp", "fsdp"), axis=1, tiled=True),
        lax.all_gather(attention_out_weight, ("dp", "fsdp"), axis=0, tiled=True),
        lax.all_gather(feedforward_in_weight, ("dp", "fsdp"), axis=0, tiled=True),
        lax.all_gather(feedforward_out_weight, ("dp", "fsdp"), axis=0, tiled=True),
    )

    def backward_step(running, slices):
        token_rows, segment, pack_cot, saved = slices
        grad_tokens, grad_down, grad_up = backward_pack(
            token_rows, segment, pack_cot, saved, back_weights, params, head_dim
        )
        return ((running[0] + grad_down, running[1] + grad_up), grad_tokens)

    starting = (
        jnp.zeros(adapter_down_factors.shape, jnp.float32),
        jnp.zeros(adapter_up_factors.shape, jnp.float32),
    )
    (down_gradient_sum, up_gradient_sum), grad_inputs = lax.scan(
        backward_step, starting, (inputs, segments, cotangent, saved_all)
    )
    finished_steps = optimizer_step_count[0].astype(jnp.float32)
    down_grand_total, up_grand_total = lax.psum(
        (down_gradient_sum, up_gradient_sum), ("dp", "fsdp")
    )
    grad_norm = jnp.sqrt(
        jnp.sum(down_grand_total * down_grand_total) + jnp.sum(up_grand_total * up_grand_total)
    )
    multiplier = jnp.minimum(1.0, clip_max / (grad_norm + 1e-06))
    revised_down, fresh_down_moment, fresh_down_square = adamw_update(
        adapter_down_factors,
        down_grand_total * multiplier,
        down_first_moment,
        down_second_moment,
        finished_steps,
        down_learning_rate,
        down_decay_factor,
    )
    revised_up, fresh_up_moment, fresh_up_square = adamw_update(
        adapter_up_factors,
        up_grand_total * multiplier,
        up_first_moment,
        up_second_moment,
        finished_steps,
        up_learning_rate,
        up_decay_factor,
    )
    return (
        outputs,
        grad_inputs,
        grad_norm,
        revised_down,
        revised_up,
        fresh_down_moment,
        fresh_up_moment,
        fresh_down_square,
        fresh_up_square,
    )


def solution(mesh):
    in_specs = (
        P(("dp", "fsdp"), None, None),
        P(("dp", "fsdp"), None),
        P(("dp", "fsdp"), None, None),
        P(None, ("dp", "fsdp"), None),
        P(("dp", "fsdp"), None),
        P(("dp", "fsdp"), None),
        P(("dp", "fsdp"), None),
        P(),
        P(),
        P(),
        P(),
        P(),
        P(),
        P(),
        P(),
        P(),
        P(),
        P(),
    )
    out_specs = (
        P(("dp", "fsdp"), None, None),
        P(("dp", "fsdp"), None, None),
        P(),
        P(),
        P(),
        P(),
        P(),
        P(),
        P(),
    )
    return jax.shard_map(shards, mesh=mesh, in_specs=in_specs, out_specs=out_specs, check_vma=False)
```

profile of v0, /device:TPU:0, one launch (start us, length us, event | category | flops | bytes accessed | tf_op | source)
XLA Modules:
  0.0 645.3 jit_solution(17930182331137238030)
XLA Ops:
  25.6 48.1 %all-gather.5.cloned.1.call-done = bf16[3,768,768]{2,1,0:T(8,128)(2,1)} async-done(((bf16[3,24,768]{2,1,0:T(8,128)(2,1)}), bf16[3,768,768]{2,1,0:T(8,128)(2,1)}) %all-gather.5.cloned.1.call-update) | async-done | bytes 3538960 | tf_op jit(solution)/shard_map/all_gather | solution.py:242
  73.7 6.0 convolution_bitcast_fusion
  86.8 78.8 %while.36 = (s32[]{:T(128)}, bf16[2,512,768]{2,1,0:T(8,128)(2,1)}, f32[2,12,512]{2,1,0:T(8,128)S(1)}, s32[2]{0:T(128)S(1)}, s32[1024]{0:T(1024)S(1)}, /*index=5*...) while((s32[]{:T(128)}, bf16[2,512,768]{2,1,0:T(8,128)(2,1)}, ...), condition=%wide.region_3.4_spmd, body=%wide.region_0.3_spmd.sunk | while | flops 1687021568 | bytes 187926752 | solution.py:80
  89.9 10.6 %fusion.136 = (f32[12,512]{1,0:T(8,128)S(1)}, f32[12,512,1024]{2,1,0:T(8,128)}) fusion(pred[512,1024]{1,0:T(8,128)(4,1)S(1)} %broadcast_compare_fusion.4, bf16[512,12,64]{0,2,1:T(8,128)(2,1)S(1)} %bitcast.167, bf16[1024,12,64]{0,2,1:T(8,128)(2,1)S(1)} %get-tuple-element.552), kind=kOutput, calls=%fused_computation.3.clone.1 | convolution fusion | flops 824174592 | bytes 28073984 | tf_op jit(solution)/shard_map/while/body/eval_jaxpr/while/body/eval_jaxpr/qhd,khd->hqk/dot_general | solution.py:66
  100.6 12.3 %fusion.137 = f32[12,512]{1,0:T(8,128)S(1)} fusion(f32[12,512,1024]{2,1,0:T(8,128)} %get-tuple-element.507, f32[12,512]{1,0:T(8,128)S(1)} %get-tuple-element.508, pred[512,1024]{1,0:T(8,128)(4,1)S(1)} %broadcast_compare_fusion.4), kind=kLoop, calls=%fused_computation.4.clone.1 | loop fusion | flops 25159680 | bytes 25739264 | tf_op jit(solution)/shard_map/while/body/eval_jaxpr/while/body/eval_jaxpr/reduce_sum | solution.py:72
  116.0 9.0 %fusion.138 = bf16[12,512,64]{1,2,0:T(8,128)(2,1)S(1)} fusion(bf16[1024,12,64]{0,2,1:T(8,128)(2,1)} %get-tuple-element.553, f32[12,512,1024]{2,1,0:T(8,128)S(1)} %copy-done, f32[12,512]{1,0:T(8,128)S(1)} %fusion.137, f32[12,512]{1,0:T(8,128)S(1)} %get-tuple-element.508, pred[512,1024]{1,0:T(8,128)(4,1)S(1)} %broadcast_compare_fusion.4), kind=kOutput, calls=%fused_computation.6.clone.1 | convolution fusion | flops 837156864 | bytes 28098560 | tf_op jit(solution)/shard_map/while/body/eval_jaxpr/while/body/eval_jaxpr/hqk,khd->qhd/dot_general | solution.py:74
  129.1 10.7 %fusion.136 = (f32[12,512]{1,0:T(8,128)S(1)}, f32[12,512,1024]{2,1,0:T(8,128)}) fusion(pred[512,1024]{1,0:T(8,128)(4,1)S(1)} %broadcast_compare_fusion.4, bf16[512,12,64]{0,2,1:T(8,128)(2,1)S(1)} %bitcast.167, bf16[1024,12,64]{0,2,1:T(8,128)(2,1)S(1)} %get-tuple-element.552), kind=kOutput, calls=%fused_computation.3.clone.1 | convolution fusion | flops 824174592 | bytes 28073984 | tf_op jit(solution)/shard_map/while/body/eval_jaxpr/while/body/eval_jaxpr/qhd,khd->hqk/dot_general | solution.py:66
  139.8 12.4 %fusion.137 = f32[12,512]{1,0:T(8,128)S(1)} fusion(f32[12,512,1024]{2,1,0:T(8,128)} %get-tuple-element.507, f32[12,512]{1,0:T(8,128)S(1)} %get-tuple-element.508, pred[512,1024]{1,0:T(8,128)(4,1)S(1)} %broadcast_compare_fusion.4), kind=kLoop, calls=%fused_computation.4.clone.1 | loop fusion | flops 25159680 | bytes 25739264 | tf_op jit(solution)/shard_map/while/body/eval_jaxpr/while/body/eval_jaxpr/reduce_sum | solution.py:72
  155.3 9.0 %fusion.138 = bf16[12,512,64]{1,2,0:T(8,128)(2,1)S(1)} fusion(bf16[1024,12,64]{0,2,1:T(8,128)(2,1)} %get-tuple-element.553, f32[12,512,1024]{2,1,0:T(8,128)S(1)} %copy-done, f32[12,512]{1,0:T(8,128)S(1)} %fusion.137, f32[12,512]{1,0:T(8,128)S(1)} %get-tuple-element.508, pred[512,1024]{1,0:T(8,128)(4,1)S(1)} %broadcast_compare_fusion.4), kind=kOutput, calls=%fused_computation.6.clone.1 | convolution fusion | flops 837156864 | bytes 28098560 | tf_op jit(solution)/shard_map/while/body/eval_jaxpr/while/body/eval_jaxpr/hqk,khd->qhd/dot_general | solution.py:74
  165.5 4.5 fusion.88
  172.1 22.9 %all-gather.9.cloned.1.call-done = bf16[768,3072]{1,0:T(8,128)(2,1)} async-done(((bf16[24,3072]{1,0:T(8,128)(2,1)}), bf16[768,3072]{1,0:T(8,128)(2,1)}) %all-gather.9.cloned.1.call-update) | async-done | bytes 4718608 | tf_op jit(solution)/shard_map/all_gather | solution.py:244
  195.0 36.9 %fusion.14 = (f32[1024,3072]{1,0:T(8,128)}, f32[1024,3072]{1,0:T(8,128)}) fusion(f32[3072]{0:T(1024)S(1)} %copy-done.44, bf16[768,3072]{1,0:T(8,128)(2,1)} %all-gather.9.cloned.1.call-done, f32[1024,768]{0,1:T(8,128)} %copy-done.12, f32[768]{0:T(1024)S(1)} %copy-done.38, f32[768]{0:T(1024)S(1)} %copy-done.37, f32[1024]{0:T(1024)S(1)} %fusion.76, ...), kind=kOutput, calls=%fused_computation.30 | convolution fusion | flops 5033951232 | bytes 33056768 | tf_op jit(solution)/shard_map/while/body/eval_jaxpr/dot_general | solution.py:24
  231.9 27.7 %all-gather.11.cloned.1.call-done = bf16[3072,768]{1,0:T(8,128)(2,1)} async-done(((bf16[96,768]{1,0:T(8,128)(2,1)}), bf16[3072,768]{1,0:T(8,128)(2,1)}) %all-gather.11.cloned.1.call-update) | async-done | bytes 4718608 | tf_op jit(solution)/shard_map/all_gather | solution.py:245
  259.7 17.9 %fusion.89 = (f32[1024]{0:T(1024)S(1)}, f32[1024,768]{0,1:T(8,128)}) fusion(f32[768]{0:T(1024)S(1)} %copy-done.39, bf16[3072,768]{1,0:T(8,128)(2,1)} %all-gather.11.cloned.1.call-done, f32[1024,3072]{1,0:T(8,128)} %get-tuple-element.392, f32[1024,3072]{1,0:T(8,128)} %get-tuple-element.393, f32[3072]{0:T(1024)S(1)} %copy-done.44, f32[768]{0:T(1024)S(1)} %copy-done.38, ...), kind=kOutput, calls=%fused_computation.153 | convolution fusion | flops 4849925120 | bytes 36209664 | tf_op jit(solution)/shard_map/while/body/eval_jaxpr/dot_general | solution.py:24
  282.8 22.1 %multiply_reduce_fusion.1 = (f32[1024]{0:T(1024)S(1)}, f32[1024,768]{0,1:T(8,128)}) fusion(f32[1024,768]{0,1:T(8,128)} %copy-done.12, f32[1024]{0:T(1024)S(1)} %broadcast_multiply_fusion.1, f32[768]{0:T(1024)S(1)} %copy-done.37, bf16[768,3072]{1,0:T(8,128)(2,1)} %all-gather.9.cloned.1.call-done, f32[1024,3072]{1,0:T(8,128)} %get-tuple-element.392, ...), kind=kOutput, calls=%fused_computation.75 | convolution fusion | flops 9728162816 | bytes 45656064 | tf_op jit(solution)/shard_map/while/body/eval_jaxpr/dot_general | solution.py:24
  304.9 4.1 fusion.87
  311.7 179.4 %while.37 = (s32[]{:T(128)}, f32[1024,12,64]{0,2,1:T(8,128)}, f32[1024,12,64]{0,2,1:T(8,128)}, bf16[2,512,768]{1,2,0:T(8,128)(2,1)}, s32[2]{0:T(128)S(1)}, /*ind...) while((s32[]{:T(128)}, f32[1024,12,64]{0,2,1:T(8,128)}, ...), condition=%wide.region_14.15_spmd.clone, body=%wide.region_12.14_spmd.clone.sunk | while | flops 4126140416 | bytes 234277232 | solution.py:134
  319.3 10.1 %fusion.149 = f32[12,512,1024]{2,1,0:T(8,128)} fusion(bf16[512,12,64]{0,2,1:T(8,128)(2,1)S(1)} %bitcast.165, bf16[1024,12,64]{0,2,1:T(8,128)(2,1)S(1)} %get-tuple-element.597), kind=kOutput, calls=%fused_computation.154.clone.1 | convolution fusion | flops 805306368 | bytes 27525120 | tf_op jit(solution)/shard_map/while/body/eval_jaxpr/while/body/eval_jaxpr/qhd,khd->hqk/dot_general | solution.py:104
  329.4 13.4 %bitcast_add_fusion.7 = f32[1024,12,64]{0,2,1:T(8,128)} fusion(f32[1024,12,64]{0,2,1:T(8,128)} %get-tuple-element.576, bf16[512,12,64]{0,2,1:T(8,128)(2,1)S(1)} %bitcast.169, f32[12,512,1024]{2,1,0:T(8,128)} %fusion.149, f32[12,512]{1,0:T(8,128)S(1)} %dynamic-slice_bitcast_fusion.2, pred[512,1024]{1,0:T(8,128)(4,1)S(1)} %broadcast_compare_fusion.5, ...), kind=kOutput, calls=%fused_computation.19.clone.1 | convolution fusion | flops 832045056 | bytes 32792576 | tf_op jit(solution)/shard_map/while/body/eval_jaxpr/while/body/eval_jaxpr/hqk,qhd->khd/dot_general | solution.py:125
  342.8 18.1 %multiply_reduce_fusion.7 = (f32[12,512]{1,0:T(8,128)S(1)}, f32[12,512,1024]{2,1,0:T(8,128)}) fusion(f32[12,512,1024]{2,1,0:T(8,128)} %fusion.149, f32[12,512]{1,0:T(8,128)S(1)} %dynamic-slice_bitcast_fusion.2, pred[512,1024]{1,0:T(8,128)(4,1)S(1)} %broadcast_compare_fusion.5, bf16[512,12,64]{0,2,1:T(8,128)(2,1)} %bitcast.168, ...), kind=kOutput, calls=%fused_computation.14.clone.1 | convolution fusion | flops 836757504 | bytes 53264384 | tf_op jit(solution)/shard_map/while/body/eval_jaxpr/while/body/eval_jaxpr/qhd,khd->hqk/dot_general | solution.py:109
  360.9 21.2 %multiply_convert_fusion.6 = bf16[12,512,1024]{2,1,0:T(8,128)(2,1)} fusion(f32[12,512,1024]{2,1,0:T(8,128)} %get-tuple-element.520, f32[12,512,1024]{2,1,0:T(8,128)} %fusion.149, f32[12,512]{1,0:T(8,128)S(1)} %get-tuple-element.521, f32[12,512]{1,0:T(8,128)S(1)} %dynamic-slice_bitcast_fusion.2, pred[512,1024]{1,0:T(8,128)(4,1)S(1)} %broadcast_compare_fusion.5), kind=kLoop, calls=%fused_computation.13.clone.1 | loop fusion | flops 37748736 | bytes 63488000 | tf_op jit(solution)/shard_map/while/body/eval_jaxpr/while/body/eval_jaxpr/convert_element_type | solution.py:113
  382.1 8.5 %convolution_multiply_fusion.2 = bf16[12,512,64]{1,2,0:T(8,128)(2,1)S(1)} fusion(bf16[12,512,1024]{2,1,0:T(8,128)(2,1)} %multiply_convert_fusion.6, bf16[1024,12,64]{0,2,1:T(8,128)(2,1)S(1)} %get-tuple-element.597), kind=kOutput, calls=%fused_computation.22.clone.1 | convolution fusion | flops 806092800 | bytes 14942208 | tf_op jit(solution)/shard_map/while/body/eval_jaxpr/while/body/eval_jaxpr/hqk,khd->qhd/dot_general | solution.py:115
  390.6 8.7 %bitcast_add_fusion.6 = f32[1024,12,64]{0,2,1:T(8,128)} fusion(f32[1024,12,64]{0,2,1:T(8,128)} %get-tuple-element.575, bf16[512,12,64]{0,2,1:T(8,128)(2,1)S(1)} %bitcast.166, bf16[12,512,1024]{2,1,0:T(8,128)(2,1)} %multiply_convert_fusion.6, pred[]{:T(512)S(6)} %compare.3), kind=kOutput, calls=%fused_computation.20.clone.1 | convolution fusion | flops 807665664 | bytes 19660800 | tf_op jit(solution)/shard_map/while/body/eval_jaxpr/while/body/eval_jaxpr/hqk,qhd->khd/dot_general | solution.py:120
  407.8 10.1 %fusion.149 = f32[12,512,1024]{2,1,0:T(8,128)} fusion(bf16[512,12,64]{0,2,1:T(8,128)(2,1)S(1)} %bitcast.165, bf16[1024,12,64]{0,2,1:T(8,128)(2,1)S(1)} %get-tuple-element.597), kind=kOutput, calls=%fused_computation.154.clone.1 | convolution fusion | flops 805306368 | bytes 27525120 | tf_op jit(solution)/shard_map/while/body/eval_jaxpr/while/body/eval_jaxpr/qhd,khd->hqk/dot_general | solution.py:104
  417.9 14.3 %bitcast_add_fusion.7 = f32[1024,12,64]{0,2,1:T(8,128)} fusion(f32[1024,12,64]{0,2,1:T(8,128)} %get-tuple-element.576, bf16[512,12,64]{0,2,1:T(8,128)(2,1)S(1)} %bitcast.169, f32[12,512,1024]{2,1,0:T(8,128)} %fusion.149, f32[12,512]{1,0:T(8,128)S(1)} %dynamic-slice_bitcast_fusion.2, pred[512,1024]{1,0:T(8,128)(4,1)S(1)} %broadcast_compare_fusion.5, ...), kind=kOutput, calls=%fused_computation.19.clone.1 | convolution fusion | flops 832045056 | bytes 32792576 | tf_op jit(solution)/shard_map/while/body/eval_jaxpr/while/body/eval_jaxpr/hqk,qhd->khd/dot_general | solution.py:125
  432.2 18.1 %multiply_reduce_fusion.7 = (f32[12,512]{1,0:T(8,128)S(1)}, f32[12,512,1024]{2,1,0:T(8,128)}) fusion(f32[12,512,1024]{2,1,0:T(8,128)} %fusion.149, f32[12,512]{1,0:T(8,128)S(1)} %dynamic-slice_bitcast_fusion.2, pred[512,1024]{1,0:T(8,128)(4,1)S(1)} %broadcast_compare_fusion.5, bf16[512,12,64]{0,2,1:T(8,128)(2,1)} %bitcast.168, ...), kind=kOutput, calls=%fused_computation.14.clone.1 | convolution fusion | flops 836757504 | bytes 53264384 | tf_op jit(solution)/shard_map/while/body/eval_jaxpr/while/body/eval_jaxpr/qhd,khd->hqk/dot_general | solution.py:109
  450.3 21.2 %multiply_convert_fusion.6 = bf16[12,512,1024]{2,1,0:T(8,128)(2,1)} fusion(f32[12,512,1024]{2,1,0:T(8,128)} %get-tuple-element.520, f32[12,512,1024]{2,1,0:T(8,128)} %fusion.149, f32[12,512]{1,0:T(8,128)S(1)} %get-tuple-element.521, f32[12,512]{1,0:T(8,128)S(1)} %dynamic-slice_bitcast_fusion.2, pred[512,1024]{1,0:T(8,128)(4,1)S(1)} %broadcast_compare_fusion.5), kind=kLoop, calls=%fused_computation.13.clone.1 | loop fusion | flops 37748736 | bytes 63488000 | tf_op jit(solution)/shard_map/while/body/eval_jaxpr/while/body/eval_jaxpr/convert_element_type | solution.py:113
  471.5 8.5 %convolution_multiply_fusion.2 = bf16[12,512,64]{1,2,0:T(8,128)(2,1)S(1)} fusion(bf16[12,512,1024]{2,1,0:T(8,128)(2,1)} %multiply_convert_fusion.6, bf16[1024,12,64]{0,2,1:T(8,128)(2,1)S(1)} %get-tuple-element.597), kind=kOutput, calls=%fused_computation.22.clone.1 | convolution fusion | flops 806092800 | bytes 14942208 | tf_op jit(solution)/shard_map/while/body/eval_jaxpr/while/body/eval_jaxpr/hqk,khd->qhd/dot_general | solution.py:115
  480.0 9.6 %bitcast_add_fusion.6 = f32[1024,12,64]{0,2,1:T(8,128)} fusion(f32[1024,12,64]{0,2,1:T(8,128)} %get-tuple-element.575, bf16[512,12,64]{0,2,1:T(8,128)(2,1)S(1)} %bitcast.166, bf16[12,512,1024]{2,1,0:T(8,128)(2,1)} %multiply_convert_fusion.6, pred[]{:T(512)S(6)} %compare.3), kind=kOutput, calls=%fused_computation.20.clone.1 | convolution fusion | flops 807665664 | bytes 19660800 | tf_op jit(solution)/shard_map/while/body/eval_jaxpr/while/body/eval_jaxpr/hqk,qhd->khd/dot_general | solution.py:120
  508.7 10.4 %fusion.37 = f32[1,1024,768]{1,2,0:T(8,128)} fusion(f32[1024,768,1]{0,1,2:T(8,128)} %fusion.73, f32[1024,768]{0,1:T(8,128)} %copy-done.14, bf16[3,768,768]{2,1,0:T(8,128)(2,1)} %all-gather.5.cloned.1.call-done, bf16[1,1024,768]{2,1,0:T(8,128)(2,1)} %copy.48, bf16[1,1024,768]{2,1,0:T(8,128)(2,1)} %copy.47, bf16[1,1024,768]{2,1,0:T(8,128)(2,1)S(1)} %bitcast.178, ...), kind=kOutput, calls=%fused_computation.73 | convolution fusion | flops 3630956544 | bytes 17698816 | tf_op jit(solution)/shard_map/while/body/eval_jaxpr/gte,gde->td/dot_general | solution.py:211
  520.6 3.6 copy.54
  524.2 106.1 %all-reduce.3.cloned.1.call-done = (f32[2,768,8]{1,2,0:T(8,128)}, f32[2,8,768]{2,1,0:T(8,128)}) async-done(((f32[2,768,8]{1,2,0:T(8,128)}, f32[2,8,768]{2,1,0:T(8,128)}), (f32[2,768,8]{1,2,0:T(8,128)}, f32[2,8,768]{2,1,0:T(8,128)})) %all-reduce.3.cloned.1.call-update) | async-done | bytes 98320 | tf_op jit(solution)/shard_map/psum | solution.py:285
  (184 shorter events, 84.1 us)
Async XLA Ops:
  7.2 10.6 %copy-start.7 = (bf16[1,1024,768]{2,1,0:T(8,128)(2,1)S(1)}, bf16[1,1024,768]{2,1,0:T(8,128)(2,1)}, u32[]{:S(2)}) copy-start(bf16[1,1024,768]{2,1,0:T(8,128)(2,1)} %param.22) | copy-start | bytes 4718596
  7.2 10.6 %copy-start.23 = (f32[2,768,8]{1,2,0:T(8,128)S(1)}, f32[2,768,8]{1,2,0:T(8,128)}, u32[]{:S(2)}) copy-start(f32[2,768,8]{1,2,0:T(8,128)} %param.33) | copy-start | bytes 147460
  7.2 11.1 %copy-start.15 = (bf16[1,1024,768]{2,1,0:T(8,128)(2,1)S(1)}, bf16[1,1024,768]{2,1,0:T(8,128)(2,1)}, u32[]{:S(2)}) copy-start(bf16[1,1024,768]{2,1,0:T(8,128)(2,1)} %param.24) | copy-start | bytes 4718596
  7.2 66.5 %all-gather.5.cloned.1.call-start = ((), (), s32[]{:S(2)}) async-start(), calls=%async_computation | async-start | bytes 3649536 | tf_op jit(solution)/shard_map/all_gather | solution.py:242
  7.9 157.6 %all-gather.7.cloned.1.call-start = ((), (), s32[]{:S(2)}) async-start(), calls=%async_computation.1 | async-start | bytes 1216512 | tf_op jit(solution)/shard_map/all_gather | solution.py:243
  8.7 186.3 %all-gather.9.cloned.1.call-start = ((), (), s32[]{:S(2)}) async-start(), calls=%async_computation.2 | async-start | bytes 4866048 | tf_op jit(solution)/shard_map/all_gather | solution.py:244
  9.4 250.2 %all-gather.11.cloned.1.call-start = ((), (), s32[]{:S(2)}) async-start(), calls=%async_computation.3 | async-start | bytes 4866048 | tf_op jit(solution)/shard_map/all_gather | solution.py:245
  10.0 620.3 %all-reduce.3.cloned.1.call-start = ((), (), s32[]{:S(2)}) async-start(), calls=%async_computation.4 | async-start | bytes 196608 | tf_op jit(solution)/shard_map/psum | solution.py:285
  86.8 78.8 %copy-start.40 = (f32[768]{0:T(1024)S(1)}, f32[768]{0:T(1024)}, u32[]{:S(2)}) copy-start(f32[768]{0:T(1024)} %get-tuple-element.329) | copy-start | bytes 9220
  100.6 15.4 %copy-start = (f32[12,512,1024]{2,1,0:T(8,128)S(1)}, f32[12,512,1024]{2,1,0:T(8,128)}, u32[]{:S(2)}) copy-start(f32[12,512,1024]{2,1,0:T(8,128)} %get-tuple-element.507) | copy-start | bytes 75497472 | tf_op jit(solution)/shard_map/while/body/eval_jaxpr/while
  139.8 15.5 %copy-start = (f32[12,512,1024]{2,1,0:T(8,128)S(1)}, f32[12,512,1024]{2,1,0:T(8,128)}, u32[]{:S(2)}) copy-start(f32[12,512,1024]{2,1,0:T(8,128)} %get-tuple-element.507) | copy-start | bytes 75497472 | tf_op jit(solution)/shard_map/while/body/eval_jaxpr/while
  165.5 4.5 copy-start.1
  165.5 4.5 copy-start.25
  170.1 24.9 %copy-start.37 = (f32[768]{0:T(1024)S(1)}, f32[768]{0:T(1024)}, u32[]{:S(2)}) copy-start(f32[768]{0:T(1024)} %get-tuple-element.331) | copy-start | bytes 9220
  170.1 24.9 %copy-start.38 = (f32[768]{0:T(1024)S(1)}, f32[768]{0:T(1024)}, u32[]{:S(2)}) copy-start(f32[768]{0:T(1024)} %get-tuple-element.333) | copy-start | bytes 9220
  170.1 24.9 %copy-start.44 = (f32[3072]{0:T(1024)S(1)}, f32[3072]{0:T(1024)}, u32[]{:S(2)}) copy-start(f32[3072]{0:T(1024)} %param.30) | copy-start | bytes 36868
  195.0 64.6 %copy-start.39 = (f32[768]{0:T(1024)S(1)}, f32[768]{0:T(1024)}, u32[]{:S(2)}) copy-start(f32[768]{0:T(1024)} %get-tuple-element.326) | copy-start | bytes 9220
  259.6 17.9 %copy-start.9 = (bf16[1,1024,768]{1,2,0:T(8,128)(2,1)S(1)}, bf16[1,1024,768]{1,2,0:T(8,128)(2,1)}, u32[]{:S(2)}) copy-start(bf16[1,1024,768]{1,2,0:T(8,128)(2,1)} %copy.44) | copy-start | bytes 4718596
  259.6 17.9 %copy-start.35 = (f32[768]{0:T(1024)S(1)}, f32[768]{0:T(1024)}, u32[]{:S(2)}) copy-start(f32[768]{0:T(1024)} %get-tuple-element.330) | copy-start | bytes 9220
  319.3 10.1 %copy-start.4 = (bf16[512,768]{0,1:T(8,128)(2,1)S(1)}, bf16[512,768]{0,1:T(8,128)(2,1)}, u32[]{:S(2)}) copy-start(bf16[512,768]{0,1:T(8,128)(2,1)} %copy.71) | copy-start | bytes 2359300 | tf_op jit(solution)/shard_map/while/body/eval_jaxpr/while
  390.6 8.7 %copy-start.16 = (bf16[2,512,768]{1,2,0:T(8,128)(2,1)S(1)}, bf16[2,512,768]{1,2,0:T(8,128)(2,1)}, u32[]{:S(2)}) copy-start(bf16[2,512,768]{1,2,0:T(8,128)(2,1)} %get-tuple-element.577) | copy-start | bytes 4718596 | tf_op jit(solution)/shard_map/while/body/eval_jaxpr/while
  407.8 10.1 %copy-start.4 = (bf16[512,768]{0,1:T(8,128)(2,1)S(1)}, bf16[512,768]{0,1:T(8,128)(2,1)}, u32[]{:S(2)}) copy-start(bf16[512,768]{0,1:T(8,128)(2,1)} %copy.71) | copy-start | bytes 2359300 | tf_op jit(solution)/shard_map/while/body/eval_jaxpr/while
  480.0 9.6 %copy-start.16 = (bf16[2,512,768]{1,2,0:T(8,128)(2,1)S(1)}, bf16[2,512,768]{1,2,0:T(8,128)(2,1)}, u32[]{:S(2)}) copy-start(bf16[2,512,768]{1,2,0:T(8,128)(2,1)} %get-tuple-element.577) | copy-start | bytes 4718596 | tf_op jit(solution)/shard_map/while/body/eval_jaxpr/while
  492.8 7.0 %copy-start.18 = (bf16[2,512,768]{2,1,0:T(8,128)(2,1)}, bf16[2,512,768]{2,1,0:T(8,128)(2,1)S(1)}, u32[]{:S(2)}) copy-start(bf16[2,512,768]{2,1,0:T(8,128)(2,1)S(1)} %copy.46) | copy-start | bytes 4718596
  492.9 4.3 copy-start.30
  495.6 4.3 copy-start.28
  504.5 4.1 copy-start.42
  508.6 10.4 %copy-start.13 = (bf16[1,1024,768]{1,2,0:T(8,128)(2,1)S(1)}, bf16[1,1024,768]{1,2,0:T(8,128)(2,1)}, u32[]{:S(2)}) copy-start(bf16[1,1024,768]{1,2,0:T(8,128)(2,1)} %get-tuple-element.387) | copy-start | bytes 4718596
  520.6 113.9 %copy-start.31 = (f32[2,768,8]{1,2,0:T(8,128)S(1)}, f32[2,768,8]{1,2,0:T(8,128)}, u32[]{:S(2)}) copy-start(f32[2,768,8]{1,2,0:T(8,128)} %param.37) | copy-start | bytes 147460
  520.6 113.9 %copy-start.32 = (f32[2,768,8]{1,2,0:T(8,128)S(1)}, f32[2,768,8]{1,2,0:T(8,128)}, u32[]{:S(2)}) copy-start(f32[2,768,8]{1,2,0:T(8,128)} %param.35) | copy-start | bytes 147460
  520.6 115.4 %copy-start.33 = (f32[2,8,768]{2,1,0:T(8,128)S(1)}, f32[2,8,768]{2,1,0:T(8,128)}, u32[]{:S(2)}) copy-start(f32[2,8,768]{2,1,0:T(8,128)} %param.38) | copy-start | bytes 147460
  520.6 115.4 %copy-start.34 = (f32[2,8,768]{2,1,0:T(8,128)S(1)}, f32[2,8,768]{2,1,0:T(8,128)}, u32[]{:S(2)}) copy-start(f32[2,8,768]{2,1,0:T(8,128)} %param.36) | copy-start | bytes 147460
  (22 other events, 54.1 us)
Sparse Core Ops, SparseCore 0:
  10.9 62.7 all-gather.4
  76.7 52.9 all-gather.6
  132.6 62.3 all-gather.8
  197.8 61.8 all-gather.10
  508.7 121.4 all-reduce.2
where the time goes:
time: 653 us; the launch traced here: 645 us
  matrix products  267 us (41%)
  waiting for transfers between devices  207 us (32%)
  other arithmetic  93.2 us (14%)
  local copies, waits for them, and re-layouts  51.9 us (8%)
  between operations  17.7 us (3%)
  loops' own time  7.52 us (1%)
    psum x1, waiting for transfers between devices, shards(): lax.psum((down_gradient_sum, up_gradient_sum), ('dp', 'fsdp'))  106 us
    dot_general x5, matrix products, matmul(): return jnp.dot(left, right, preferred_element_type=jnp.float32)  84 us
    all_gather x1, waiting for transfers between devices, shards(): lax.all_gather(query_key_value_weight, ('dp', 'fsdp'), axis=1, tiled=True)  48.1 us
    convert_element_type x2, other arithmetic, one_block(): grad_scores = (soft_weights * (grad_soft - row_inner)).astype(jnp.bfloat16)  42.4 us
    dot_general x4, matrix products, one_block(): jnp.einsum('qhd,khd->hqk', query_block, key_heads, preferred_element_type...  41.5 us
    dot_general x2, matrix products, one_block(): jnp.einsum('qhd,khd->hqk', grad_block, value_heads, preferred_element_typ...  36.2 us
    all_gather x1, waiting for transfers between devices, shards(): lax.all_gather(feedforward_out_weight, ('dp', 'fsdp'), axis=0, tiled=True)  27.7 us
    dot_general x2, matrix products, one_block(): jnp.einsum('hqk,qhd->khd', soft_weights.astype(jnp.bfloat16), grad_block,...  27.7 us
  transfers between devices with their start and end apart: 5, of which 4 were waited for; matrix products, arithmetic and copies ran while one was open for 23% of the time, Pallas kernels for 0%

commit v1 on v0

--- a/solution.py
+++ b/solution.py
@@ -1,3 +1,5 @@
+import functools
+
 import jax
 import jax.numpy as jnp
 from jax import lax
@@ -217,7 +219,24 @@
     return (grad_tokens, grad_down, grad_up)
 
 
+def flip(values, axis, bit, size):
+    return lax.ppermute(values, axis, [(index, index ^ bit) for index in range(size)])
+
+
+def butterfly_sum(values, sizes):
+    for axis, size in sizes:
+        if size & (size - 1):
+            values = lax.psum(values, axis)
+            continue
+        bit = 1
+        while bit < size:
+            values = values + flip(values, axis, bit, size)
+            bit *= 2
+    return values
+
+
 def shards(
+    sizes,
     inputs,
     segments,
     cotangent,
@@ -282,9 +301,12 @@
         backward_step, starting, (inputs, segments, cotangent, saved_all)
     )
     finished_steps = optimizer_step_count[0].astype(jnp.float32)
-    down_grand_total, up_grand_total = lax.psum(
-        (down_gradient_sum, up_gradient_sum), ("dp", "fsdp")
-    )
+    packed = jnp.concatenate(
+        [jnp.swapaxes(down_gradient_sum, 1, 2), up_gradient_sum], axis=0
+    )
+    packed = butterfly_sum(packed, sizes)
+    down_grand_total = jnp.swapaxes(packed[:2], 1, 2)
+    up_grand_total = packed[2:]
     grad_norm = jnp.sqrt(
         jnp.sum(down_grand_total * down_grand_total) + jnp.sum(up_grand_total * up_grand_total)
     )
@@ -352,4 +374,5 @@
         P(),
         P(),
     )
-    return jax.shard_map(shards, mesh=mesh, in_specs=in_specs, out_specs=out_specs, check_vma=False)
+    sizes = tuple((axis, mesh.shape[axis]) for axis in ("dp", "fsdp"))
+    return jax.shard_map(functools.partial(shards, sizes), mesh=mesh, in_specs=in_specs, out_specs=out_specs, check_vma=False)

time: 653 us -> 553 us (0.85)
  waiting for transfers between devices: 207 us -> 110 us
    psum x1 -> x0, waiting for transfers between devices: 106 us -> none  [shards(): lax.psum((down_gradient_sum, up_gradient_sum), ('dp', 'fsdp'))]
    ppermute x0 -> x5, waiting for transfers between devices: none -> 7.84 us  [flip(): lax.ppermute(values, axis, [(index, index ^ bit) for index in range(size)])]
    unnamed x86 -> x82, local copies, waits for them, and re-layouts: 17.6 us -> 17.5 us
  transfers between devices with their start and end apart: 5 -> 9, of which waited for: 4 -> 7; matrix products, arithmetic and copies ran while one was open for 23% -> 28% of each run, Pallas kernels for 0% -> 0%
where the time goes in v1:
time: 553 us; the launch traced here: 546 us
  matrix products  266 us (48%)
  waiting for transfers between devices  110 us (20%)
  other arithmetic  87.8 us (16%)
  local copies, waits for them, and re-layouts  50.7 us (9%)
  between operations  17.7 us (3%)
  loops' own time  7.52 us (1%)
  starting transfers between devices  6.66 us (1%)
    dot_general x5, matrix products, matmul(): return jnp.dot(left, right, preferred_element_type=jnp.float32)  84 us
    all_gather x1, waiting for transfers between devices, shards(): lax.all_gather(query_key_value_weight, ('dp', 'fsdp'), axis=1, tiled=True)  49 us
    convert_element_type x2, other arithmetic, one_block(): grad_scores = (soft_weights * (grad_soft - row_inner)).astype(jnp.bfloat16)  42.4 us
    dot_general x4, matrix products, one_block(): jnp.einsum('qhd,khd->hqk', query_block, key_heads, preferred_element_type...  41.5 us
    dot_general x2, matrix products, one_block(): jnp.einsum('qhd,khd->hqk', grad_block, value_heads, preferred_element_typ...  36.2 us
    all_gather x1, waiting for transfers between devices, shards(): lax.all_gather(feedforward_out_weight, ('dp', 'fsdp'), axis=0, tiled=True)  27.7 us
    dot_general x2, matrix products, one_block(): jnp.einsum('hqk,qhd->khd', soft_weights.astype(jnp.bfloat16), grad_block,...  27.7 us
    reduce_sum x2, other arithmetic, one_block(): row_total = jnp.sum(exponent, axis=-1, keepdims=True)  24.7 us
  transfers between devices with their start and end apart: 9, of which 7 were waited for; matrix products, arithmetic and copies ran while one was open for 28% of the time, Pallas kernels for 0%

profile of v1, /device:TPU:0, one launch (start us, length us, event | category | flops | bytes accessed | tf_op | source)
XLA Modules:
  0.0 546.5 jit_solution(6162718479515744584)
XLA Ops:
  24.8 49.0 %all-gather.5.cloned.1.call-done = bf16[3,768,768]{2,1,0:T(8,128)(2,1)} async-done(((bf16[3,24,768]{2,1,0:T(8,128)(2,1)}), bf16[3,768,768]{2,1,0:T(8,128)(2,1)}) %all-gather.5.cloned.1.call-update) | async-done | bytes 3538960 | tf_op jit(solution)/shard_map/all_gather | solution.py:261
  73.8 6.0 %convolution_bitcast_fusion = f32[3,1024,768]{1,2,0:T(8,128)S(1)} fusion(bf16[3,768,768]{2,1,0:T(8,128)(2,1)} %all-gather.5.cloned.1.call-done, bf16[1,1024,768]{2,1,0:T(8,128)(2,1)S(1)} %copy-done.7), kind=kOutput, calls=%fused_computation.58 | convolution fusion | flops 3623878656 | bytes 14548992 | tf_op jit(solution)/shard_map/while/body/eval_jaxpr/td,gde->gte/dot_general | solution.py:155
  86.8 78.8 %while.36 = (s32[]{:T(128)}, bf16[2,512,768]{2,1,0:T(8,128)(2,1)}, f32[2,12,512]{2,1,0:T(8,128)S(1)}, s32[2]{0:T(128)S(1)}, s32[1024]{0:T(1024)S(1)}, /*index=5*...) while((s32[]{:T(128)}, bf16[2,512,768]{2,1,0:T(8,128)(2,1)}, ...), condition=%wide.region_3.4_spmd, body=%wide.region_0.3_spmd.sunk | while | flops 1687021568 | bytes 187926752 | solution.py:82
  90.0 10.7 %fusion.136 = (f32[12,512]{1,0:T(8,128)S(1)}, f32[12,512,1024]{2,1,0:T(8,128)}) fusion(pred[512,1024]{1,0:T(8,128)(4,1)S(1)} %broadcast_compare_fusion.4, bf16[512,12,64]{0,2,1:T(8,128)(2,1)S(1)} %bitcast.170, bf16[1024,12,64]{0,2,1:T(8,128)(2,1)S(1)} %get-tuple-element.552), kind=kOutput, calls=%fused_computation.3.clone.1 | convolution fusion | flops 824174592 | bytes 28073984 | tf_op jit(solution)/shard_map/while/body/eval_jaxpr/while/body/eval_jaxpr/qhd,khd->hqk/dot_general | solution.py:68
  100.7 12.3 %fusion.137 = f32[12,512]{1,0:T(8,128)S(1)} fusion(f32[12,512,1024]{2,1,0:T(8,128)} %get-tuple-element.507, f32[12,512]{1,0:T(8,128)S(1)} %get-tuple-element.508, pred[512,1024]{1,0:T(8,128)(4,1)S(1)} %broadcast_compare_fusion.4), kind=kLoop, calls=%fused_computation.4.clone.1 | loop fusion | flops 25159680 | bytes 25739264 | tf_op jit(solution)/shard_map/while/body/eval_jaxpr/while/body/eval_jaxpr/reduce_sum | solution.py:74
  116.1 9.0 %fusion.138 = bf16[12,512,64]{1,2,0:T(8,128)(2,1)S(1)} fusion(bf16[1024,12,64]{0,2,1:T(8,128)(2,1)} %get-tuple-element.553, f32[12,512,1024]{2,1,0:T(8,128)S(1)} %copy-done, f32[12,512]{1,0:T(8,128)S(1)} %fusion.137, f32[12,512]{1,0:T(8,128)S(1)} %get-tuple-element.508, pred[512,1024]{1,0:T(8,128)(4,1)S(1)} %broadcast_compare_fusion.4), kind=kOutput, calls=%fused_computation.6.clone.1 | convolution fusion | flops 837156864 | bytes 28098560 | tf_op jit(solution)/shard_map/while/body/eval_jaxpr/while/body/eval_jaxpr/hqk,khd->qhd/dot_general | solution.py:76
  129.2 10.7 %fusion.136 = (f32[12,512]{1,0:T(8,128)S(1)}, f32[12,512,1024]{2,1,0:T(8,128)}) fusion(pred[512,1024]{1,0:T(8,128)(4,1)S(1)} %broadcast_compare_fusion.4, bf16[512,12,64]{0,2,1:T(8,128)(2,1)S(1)} %bitcast.170, bf16[1024,12,64]{0,2,1:T(8,128)(2,1)S(1)} %get-tuple-element.552), kind=kOutput, calls=%fused_computation.3.clone.1 | convolution fusion | flops 824174592 | bytes 28073984 | tf_op jit(solution)/shard_map/while/body/eval_jaxpr/while/body/eval_jaxpr/qhd,khd->hqk/dot_general | solution.py:68
  139.9 12.4 %fusion.137 = f32[12,512]{1,0:T(8,128)S(1)} fusion(f32[12,512,1024]{2,1,0:T(8,128)} %get-tuple-element.507, f32[12,512]{1,0:T(8,128)S(1)} %get-tuple-element.508, pred[512,1024]{1,0:T(8,128)(4,1)S(1)} %broadcast_compare_fusion.4), kind=kLoop, calls=%fused_computation.4.clone.1 | loop fusion | flops 25159680 | bytes 25739264 | tf_op jit(solution)/shard_map/while/body/eval_jaxpr/while/body/eval_jaxpr/reduce_sum | solution.py:74
  155.4 9.0 %fusion.138 = bf16[12,512,64]{1,2,0:T(8,128)(2,1)S(1)} fusion(bf16[1024,12,64]{0,2,1:T(8,128)(2,1)} %get-tuple-element.553, f32[12,512,1024]{2,1,0:T(8,128)S(1)} %copy-done, f32[12,512]{1,0:T(8,128)S(1)} %fusion.137, f32[12,512]{1,0:T(8,128)S(1)} %get-tuple-element.508, pred[512,1024]{1,0:T(8,128)(4,1)S(1)} %broadcast_compare_fusion.4), kind=kOutput, calls=%fused_computation.6.clone.1 | convolution fusion | flops 837156864 | bytes 28098560 | tf_op jit(solution)/shard_map/while/body/eval_jaxpr/while/body/eval_jaxpr/hqk,khd->qhd/dot_general | solution.py:76
  165.7 4.5 fusion.88
  172.3 22.9 %all-gather.9.cloned.1.call-done = bf16[768,3072]{1,0:T(8,128)(2,1)} async-done(((bf16[24,3072]{1,0:T(8,128)(2,1)}), bf16[768,3072]{1,0:T(8,128)(2,1)}) %all-gather.9.cloned.1.call-update) | async-done | bytes 4718608 | tf_op jit(solution)/shard_map/all_gather | solution.py:263
  195.1 36.9 %fusion.14 = (f32[1024,3072]{1,0:T(8,128)}, f32[1024,3072]{1,0:T(8,128)}) fusion(f32[3072]{0:T(1024)S(1)} %copy-done.42, bf16[768,3072]{1,0:T(8,128)(2,1)} %all-gather.9.cloned.1.call-done, f32[1024,768]{0,1:T(8,128)} %copy-done.12, f32[768]{0:T(1024)S(1)} %copy-done.36, f32[768]{0:T(1024)S(1)} %copy-done.35, f32[1024]{0:T(1024)S(1)} %fusion.74, ...), kind=kOutput, calls=%fused_computation.30 | convolution fusion | flops 5033951232 | bytes 33056768 | tf_op jit(solution)/shard_map/while/body/eval_jaxpr/dot_general | solution.py:26
  232.0 27.7 %all-gather.11.cloned.1.call-done = bf16[3072,768]{1,0:T(8,128)(2,1)} async-done(((bf16[96,768]{1,0:T(8,128)(2,1)}), bf16[3072,768]{1,0:T(8,128)(2,1)}) %all-gather.11.cloned.1.call-update) | async-done | bytes 4718608 | tf_op jit(solution)/shard_map/all_gather | solution.py:264
  259.8 17.9 %fusion.89 = (f32[1024]{0:T(1024)S(1)}, f32[1024,768]{0,1:T(8,128)}) fusion(f32[768]{0:T(1024)S(1)} %copy-done.37, bf16[3072,768]{1,0:T(8,128)(2,1)} %all-gather.11.cloned.1.call-done, f32[1024,3072]{1,0:T(8,128)} %get-tuple-element.392, f32[1024,3072]{1,0:T(8,128)} %get-tuple-element.393, f32[3072]{0:T(1024)S(1)} %copy-done.42, f32[768]{0:T(1024)S(1)} %copy-done.36, ...), kind=kOutput, calls=%fused_computation.157 | convolution fusion | flops 4849925120 | bytes 36209664 | tf_op jit(solution)/shard_map/while/body/eval_jaxpr/dot_general | solution.py:26
  282.9 22.1 %multiply_reduce_fusion.1 = (f32[1024]{0:T(1024)S(1)}, f32[1024,768]{0,1:T(8,128)}) fusion(f32[1024,768]{0,1:T(8,128)} %copy-done.12, f32[1024]{0:T(1024)S(1)} %broadcast_multiply_fusion.1, f32[768]{0:T(1024)S(1)} %copy-done.35, bf16[768,3072]{1,0:T(8,128)(2,1)} %all-gather.9.cloned.1.call-done, f32[1024,3072]{1,0:T(8,128)} %get-tuple-element.392, ...), kind=kOutput, calls=%fused_computation.75 | convolution fusion | flops 9728162816 | bytes 45656064 | tf_op jit(solution)/shard_map/while/body/eval_jaxpr/dot_general | solution.py:26
  305.0 4.1 fusion.87
  311.8 179.4 %while.37 = (s32[]{:T(128)}, f32[1024,12,64]{0,2,1:T(8,128)}, f32[1024,12,64]{0,2,1:T(8,128)}, bf16[2,512,768]{1,2,0:T(8,128)(2,1)}, s32[2]{0:T(128)S(1)}, /*ind...) while((s32[]{:T(128)}, f32[1024,12,64]{0,2,1:T(8,128)}, ...), condition=%wide.region_14.15_spmd.clone, body=%wide.region_12.14_spmd.clone.sunk | while | flops 4126140416 | bytes 234277232 | solution.py:136
  319.4 10.1 %fusion.149 = f32[12,512,1024]{2,1,0:T(8,128)} fusion(bf16[512,12,64]{0,2,1:T(8,128)(2,1)S(1)} %bitcast.168, bf16[1024,12,64]{0,2,1:T(8,128)(2,1)S(1)} %get-tuple-element.597), kind=kOutput, calls=%fused_computation.158.clone.1 | convolution fusion | flops 805306368 | bytes 27525120 | tf_op jit(solution)/shard_map/while/body/eval_jaxpr/while/body/eval_jaxpr/qhd,khd->hqk/dot_general | solution.py:106
  329.5 13.4 %bitcast_add_fusion.7 = f32[1024,12,64]{0,2,1:T(8,128)} fusion(f32[1024,12,64]{0,2,1:T(8,128)} %get-tuple-element.576, bf16[512,12,64]{0,2,1:T(8,128)(2,1)S(1)} %bitcast.172, f32[12,512,1024]{2,1,0:T(8,128)} %fusion.149, f32[12,512]{1,0:T(8,128)S(1)} %dynamic-slice_bitcast_fusion.2, pred[512,1024]{1,0:T(8,128)(4,1)S(1)} %broadcast_compare_fusion.5, ...), kind=kOutput, calls=%fused_computation.19.clone.1 | convolution fusion | flops 832045056 | bytes 32792576 | tf_op jit(solution)/shard_map/while/body/eval_jaxpr/while/body/eval_jaxpr/hqk,qhd->khd/dot_general | solution.py:127
  342.9 18.1 %multiply_reduce_fusion.7 = (f32[12,512]{1,0:T(8,128)S(1)}, f32[12,512,1024]{2,1,0:T(8,128)}) fusion(f32[12,512,1024]{2,1,0:T(8,128)} %fusion.149, f32[12,512]{1,0:T(8,128)S(1)} %dynamic-slice_bitcast_fusion.2, pred[512,1024]{1,0:T(8,128)(4,1)S(1)} %broadcast_compare_fusion.5, bf16[512,12,64]{0,2,1:T(8,128)(2,1)} %bitcast.171, ...), kind=kOutput, calls=%fused_computation.14.clone.1 | convolution fusion | flops 836757504 | bytes 53264384 | tf_op jit(solution)/shard_map/while/body/eval_jaxpr/while/body/eval_jaxpr/qhd,khd->hqk/dot_general | solution.py:111
  361.0 21.2 %multiply_convert_fusion.6 = bf16[12,512,1024]{2,1,0:T(8,128)(2,1)} fusion(f32[12,512,1024]{2,1,0:T(8,128)} %get-tuple-element.520, f32[12,512,1024]{2,1,0:T(8,128)} %fusion.149, f32[12,512]{1,0:T(8,128)S(1)} %get-tuple-element.521, f32[12,512]{1,0:T(8,128)S(1)} %dynamic-slice_bitcast_fusion.2, pred[512,1024]{1,0:T(8,128)(4,1)S(1)} %broadcast_compare_fusion.5), kind=kLoop, calls=%fused_computation.13.clone.1 | loop fusion | flops 37748736 | bytes 63488000 | tf_op jit(solution)/shard_map/while/body/eval_jaxpr/while/body/eval_jaxpr/convert_element_type | solution.py:115
  382.2 8.5 %convolution_multiply_fusion.2 = bf16[12,512,64]{1,2,0:T(8,128)(2,1)S(1)} fusion(bf16[12,512,1024]{2,1,0:T(8,128)(2,1)} %multiply_convert_fusion.6, bf16[1024,12,64]{0,2,1:T(8,128)(2,1)S(1)} %get-tuple-element.597), kind=kOutput, calls=%fused_computation.22.clone.1 | convolution fusion | flops 806092800 | bytes 14942208 | tf_op jit(solution)/shard_map/while/body/eval_jaxpr/while/body/eval_jaxpr/hqk,khd->qhd/dot_general | solution.py:117
  390.7 8.7 %bitcast_add_fusion.6 = f32[1024,12,64]{0,2,1:T(8,128)} fusion(f32[1024,12,64]{0,2,1:T(8,128)} %get-tuple-element.575, bf16[512,12,64]{0,2,1:T(8,128)(2,1)S(1)} %bitcast.169, bf16[12,512,1024]{2,1,0:T(8,128)(2,1)} %multiply_convert_fusion.6, pred[]{:T(512)S(6)} %compare.3), kind=kOutput, calls=%fused_computation.20.clone.1 | convolution fusion | flops 807665664 | bytes 19660800 | tf_op jit(solution)/shard_map/while/body/eval_jaxpr/while/body/eval_jaxpr/hqk,qhd->khd/dot_general | solution.py:122
  407.9 10.1 %fusion.149 = f32[12,512,1024]{2,1,0:T(8,128)} fusion(bf16[512,12,64]{0,2,1:T(8,128)(2,1)S(1)} %bitcast.168, bf16[1024,12,64]{0,2,1:T(8,128)(2,1)S(1)} %get-tuple-element.597), kind=kOutput, calls=%fused_computation.158.clone.1 | convolution fusion | flops 805306368 | bytes 27525120 | tf_op jit(solution)/shard_map/while/body/eval_jaxpr/while/body/eval_jaxpr/qhd,khd->hqk/dot_general | solution.py:106
  418.0 14.3 %bitcast_add_fusion.7 = f32[1024,12,64]{0,2,1:T(8,128)} fusion(f32[1024,12,64]{0,2,1:T(8,128)} %get-tuple-element.576, bf16[512,12,64]{0,2,1:T(8,128)(2,1)S(1)} %bitcast.172, f32[12,512,1024]{2,1,0:T(8,128)} %fusion.149, f32[12,512]{1,0:T(8,128)S(1)} %dynamic-slice_bitcast_fusion.2, pred[512,1024]{1,0:T(8,128)(4,1)S(1)} %broadcast_compare_fusion.5, ...), kind=kOutput, calls=%fused_computation.19.clone.1 | convolution fusion | flops 832045056 | bytes 32792576 | tf_op jit(solution)/shard_map/while/body/eval_jaxpr/while/body/eval_jaxpr/hqk,qhd->khd/dot_general | solution.py:127
  432.3 18.1 %multiply_reduce_fusion.7 = (f32[12,512]{1,0:T(8,128)S(1)}, f32[12,512,1024]{2,1,0:T(8,128)}) fusion(f32[12,512,1024]{2,1,0:T(8,128)} %fusion.149, f32[12,512]{1,0:T(8,128)S(1)} %dynamic-slice_bitcast_fusion.2, pred[512,1024]{1,0:T(8,128)(4,1)S(1)} %broadcast_compare_fusion.5, bf16[512,12,64]{0,2,1:T(8,128)(2,1)} %bitcast.171, ...), kind=kOutput, calls=%fused_computation.14.clone.1 | convolution fusion | flops 836757504 | bytes 53264384 | tf_op jit(solution)/shard_map/while/body/eval_jaxpr/while/body/eval_jaxpr/qhd,khd->hqk/dot_general | solution.py:111
  450.4 21.2 %multiply_convert_fusion.6 = bf16[12,512,1024]{2,1,0:T(8,128)(2,1)} fusion(f32[12,512,1024]{2,1,0:T(8,128)} %get-tuple-element.520, f32[12,512,1024]{2,1,0:T(8,128)} %fusion.149, f32[12,512]{1,0:T(8,128)S(1)} %get-tuple-element.521, f32[12,512]{1,0:T(8,128)S(1)} %dynamic-slice_bitcast_fusion.2, pred[512,1024]{1,0:T(8,128)(4,1)S(1)} %broadcast_compare_fusion.5), kind=kLoop, calls=%fused_computation.13.clone.1 | loop fusion | flops 37748736 | bytes 63488000 | tf_op jit(solution)/shard_map/while/body/eval_jaxpr/while/body/eval_jaxpr/convert_element_type | solution.py:115
  471.6 8.5 %convolution_multiply_fusion.2 = bf16[12,512,64]{1,2,0:T(8,128)(2,1)S(1)} fusion(bf16[12,512,1024]{2,1,0:T(8,128)(2,1)} %multiply_convert_fusion.6, bf16[1024,12,64]{0,2,1:T(8,128)(2,1)S(1)} %get-tuple-element.597), kind=kOutput, calls=%fused_computation.22.clone.1 | convolution fusion | flops 806092800 | bytes 14942208 | tf_op jit(solution)/shard_map/while/body/eval_jaxpr/while/body/eval_jaxpr/hqk,khd->qhd/dot_general | solution.py:117
  480.1 9.6 %bitcast_add_fusion.6 = f32[1024,12,64]{0,2,1:T(8,128)} fusion(f32[1024,12,64]{0,2,1:T(8,128)} %get-tuple-element.575, bf16[512,12,64]{0,2,1:T(8,128)(2,1)S(1)} %bitcast.169, bf16[12,512,1024]{2,1,0:T(8,128)(2,1)} %multiply_convert_fusion.6, pred[]{:T(512)S(6)} %compare.3), kind=kOutput, calls=%fused_computation.20.clone.1 | convolution fusion | flops 807665664 | bytes 19660800 | tf_op jit(solution)/shard_map/while/body/eval_jaxpr/while/body/eval_jaxpr/hqk,qhd->khd/dot_general | solution.py:122
  503.4 3.5 collective-permute-done.1
  519.8 10.3 %fusion.37 = f32[1,1024,768]{1,2,0:T(8,128)} fusion(f32[1024,768,1]{0,1,2:T(8,128)} %fusion.71, f32[1024,768]{0,1:T(8,128)} %copy-done.14, bf16[3,768,768]{2,1,0:T(8,128)(2,1)} %all-gather.5.cloned.1.call-done, bf16[1,1024,768]{2,1,0:T(8,128)(2,1)} %copy.48, bf16[1,1024,768]{2,1,0:T(8,128)(2,1)} %copy.47, bf16[1,1024,768]{2,1,0:T(8,128)(2,1)S(1)} %bitcast.181, ...), kind=kOutput, calls=%fused_computation.73 | convolution fusion | flops 3630956544 | bytes 17698816 | tf_op jit(solution)/shard_map/while/body/eval_jaxpr/gte,gde->td/dot_general | solution.py:213
  531.7 3.6 copy.54
  (192 shorter events, 87.1 us)
Async XLA Ops:
  7.2 9.8 %copy-start.7 = (bf16[1,1024,768]{2,1,0:T(8,128)(2,1)S(1)}, bf16[1,1024,768]{2,1,0:T(8,128)(2,1)}, u32[]{:S(2)}) copy-start(bf16[1,1024,768]{2,1,0:T(8,128)(2,1)} %param.22) | copy-start | bytes 4718596
  7.2 9.8 %copy-start.21 = (f32[2,768,8]{1,2,0:T(8,128)S(1)}, f32[2,768,8]{1,2,0:T(8,128)}, u32[]{:S(2)}) copy-start(f32[2,768,8]{1,2,0:T(8,128)} %param.33) | copy-start | bytes 147460
  7.2 10.3 %copy-start.15 = (bf16[1,1024,768]{2,1,0:T(8,128)(2,1)S(1)}, bf16[1,1024,768]{2,1,0:T(8,128)(2,1)}, u32[]{:S(2)}) copy-start(bf16[1,1024,768]{2,1,0:T(8,128)(2,1)} %param.24) | copy-start | bytes 4718596
  7.2 66.6 %all-gather.5.cloned.1.call-start = ((), (), s32[]{:S(2)}) async-start(), calls=%async_computation | async-start | bytes 3649536 | tf_op jit(solution)/shard_map/all_gather | solution.py:261
  7.9 157.7 %all-gather.7.cloned.1.call-start = ((), (), s32[]{:S(2)}) async-start(), calls=%async_computation.1 | async-start | bytes 1216512 | tf_op jit(solution)/shard_map/all_gather | solution.py:262
  8.7 186.4 %all-gather.9.cloned.1.call-start = ((), (), s32[]{:S(2)}) async-start(), calls=%async_computation.2 | async-start | bytes 4866048 | tf_op jit(solution)/shard_map/all_gather | solution.py:263
  9.4 250.3 %all-gather.11.cloned.1.call-start = ((), (), s32[]{:S(2)}) async-start(), calls=%async_computation.3 | async-start | bytes 4866048 | tf_op jit(solution)/shard_map/all_gather | solution.py:264
  86.8 78.8 %copy-start.38 = (f32[768]{0:T(1024)S(1)}, f32[768]{0:T(1024)}, u32[]{:S(2)}) copy-start(f32[768]{0:T(1024)} %get-tuple-element.331) | copy-start | bytes 9220
  100.7 15.4 %copy-start = (f32[12,512,1024]{2,1,0:T(8,128)S(1)}, f32[12,512,1024]{2,1,0:T(8,128)}, u32[]{:S(2)}) copy-start(f32[12,512,1024]{2,1,0:T(8,128)} %get-tuple-element.507) | copy-start | bytes 75497472 | tf_op jit(solution)/shard_map/while/body/eval_jaxpr/while
  139.9 15.5 %copy-start = (f32[12,512,1024]{2,1,0:T(8,128)S(1)}, f32[12,512,1024]{2,1,0:T(8,128)}, u32[]{:S(2)}) copy-start(f32[12,512,1024]{2,1,0:T(8,128)} %get-tuple-element.507) | copy-start | bytes 75497472 | tf_op jit(solution)/shard_map/while/body/eval_jaxpr/while
  170.2 24.9 %copy-start.35 = (f32[768]{0:T(1024)S(1)}, f32[768]{0:T(1024)}, u32[]{:S(2)}) copy-start(f32[768]{0:T(1024)} %get-tuple-element.333) | copy-start | bytes 9220
  170.2 24.9 %copy-start.36 = (f32[768]{0:T(1024)S(1)}, f32[768]{0:T(1024)}, u32[]{:S(2)}) copy-start(f32[768]{0:T(1024)} %get-tuple-element.335) | copy-start | bytes 9220
  170.2 24.9 %copy-start.42 = (f32[3072]{0:T(1024)S(1)}, f32[3072]{0:T(1024)}, u32[]{:S(2)}) copy-start(f32[3072]{0:T(1024)} %param.30) | copy-start | bytes 36868
  195.1 64.6 %copy-start.37 = (f32[768]{0:T(1024)S(1)}, f32[768]{0:T(1024)}, u32[]{:S(2)}) copy-start(f32[768]{0:T(1024)} %get-tuple-element.328) | copy-start | bytes 9220
  259.7 17.9 %copy-start.9 = (bf16[1,1024,768]{1,2,0:T(8,128)(2,1)S(1)}, bf16[1,1024,768]{1,2,0:T(8,128)(2,1)}, u32[]{:S(2)}) copy-start(bf16[1,1024,768]{1,2,0:T(8,128)(2,1)} %copy.44) | copy-start | bytes 4718596
  259.8 17.9 %copy-start.33 = (f32[768]{0:T(1024)S(1)}, f32[768]{0:T(1024)}, u32[]{:S(2)}) copy-start(f32[768]{0:T(1024)} %get-tuple-element.332) | copy-start | bytes 9220
  319.4 10.1 %copy-start.4 = (bf16[512,768]{0,1:T(8,128)(2,1)S(1)}, bf16[512,768]{0,1:T(8,128)(2,1)}, u32[]{:S(2)}) copy-start(bf16[512,768]{0,1:T(8,128)(2,1)} %copy.71) | copy-start | bytes 2359300 | tf_op jit(solution)/shard_map/while/body/eval_jaxpr/while
  390.7 8.7 %copy-start.16 = (bf16[2,512,768]{1,2,0:T(8,128)(2,1)S(1)}, bf16[2,512,768]{1,2,0:T(8,128)(2,1)}, u32[]{:S(2)}) copy-start(bf16[2,512,768]{1,2,0:T(8,128)(2,1)} %get-tuple-element.577) | copy-start | bytes 4718596 | tf_op jit(solution)/shard_map/while/body/eval_jaxpr/while
  407.9 10.1 %copy-start.4 = (bf16[512,768]{0,1:T(8,128)(2,1)S(1)}, bf16[512,768]{0,1:T(8,128)(2,1)}, u32[]{:S(2)}) copy-start(bf16[512,768]{0,1:T(8,128)(2,1)} %copy.71) | copy-start | bytes 2359300 | tf_op jit(solution)/shard_map/while/body/eval_jaxpr/while
  480.1 9.6 %copy-start.16 = (bf16[2,512,768]{1,2,0:T(8,128)(2,1)S(1)}, bf16[2,512,768]{1,2,0:T(8,128)(2,1)}, u32[]{:S(2)}) copy-start(bf16[2,512,768]{1,2,0:T(8,128)(2,1)} %get-tuple-element.577) | copy-start | bytes 4718596 | tf_op jit(solution)/shard_map/while/body/eval_jaxpr/while
  498.8 14.5 %copy-start.22 = (f32[2,768,8]{1,2,0:T(8,128)S(1)}, f32[2,768,8]{1,2,0:T(8,128)}, u32[]{:S(2)}) copy-start(f32[2,768,8]{1,2,0:T(8,128)} %param.33) | copy-start | bytes 147460
  500.2 15.4 %copy-start.3 = (f32[1024,12,64]{0,2,1:T(8,128)S(1)}, f32[1024,12,64]{0,2,1:T(8,128)}, u32[]{:S(2)}) copy-start(f32[1024,12,64]{0,2,1:T(8,128)} %get-tuple-element.224) | copy-start | bytes 9437188
  500.5 1.4 collective-permute-start
  501.9 5.0 collective-permute-start.1
  506.9 4.7 collective-permute-start.2
  511.6 6.6 %collective-permute-start.3 = (f32[4,8,768]{2,1,0:T(8,128)S(1)}, f32[4,8,768]{2,1,0:T(8,128)S(1)}, u32[]{:S(2)}, u32[]{:S(2)}) collective-permute-start(f32[4,8,768]{2,1,0:T(8,128)S(1)} %add.285), channel_id=1, source_target_pairs={{0,16},{2,18},{4,20},{6,22},{8,24},{10,26},{12,28},{14,30},{16,0},... | collective-permute-start | bytes 294920 | tf_op jit(solution)/shard_map/ppermute | solution.py:223
  518.3 11.8 %copy-start.13 = (bf16[1,1024,768]{1,2,0:T(8,128)(2,1)S(1)}, bf16[1,1024,768]{1,2,0:T(8,128)(2,1)}, u32[]{:S(2)}) copy-start(bf16[1,1024,768]{1,2,0:T(8,128)(2,1)} %get-tuple-element.387) | copy-start | bytes 4718596
  518.3 16.9 %collective-permute-start.4 = (f32[4,8,768]{2,1,0:T(8,128)S(1)}, f32[4,8,768]{2,1,0:T(8,128)S(1)}, u32[]{:S(2)}, u32[]{:S(2)}) collective-permute-start(f32[4,8,768]{2,1,0:T(8,128)S(1)} %add.286), channel_id=1, source_target_pairs={{0,1},{1,0},{2,3},{3,2},{4,5},{5,4},{6,7},{7,6},{8,9},{9,8},{10,11... | collective-permute-start | bytes 294920 | tf_op jit(solution)/shard_map/ppermute | solution.py:223
  531.6 5.6 %copy-start.29 = (f32[2,8,768]{2,1,0:T(8,128)S(1)}, f32[2,8,768]{2,1,0:T(8,128)}, u32[]{:S(2)}) copy-start(f32[2,8,768]{2,1,0:T(8,128)} %param.38) | copy-start | bytes 147460
  531.6 5.6 %copy-start.30 = (f32[2,8,768]{2,1,0:T(8,128)S(1)}, f32[2,8,768]{2,1,0:T(8,128)}, u32[]{:S(2)}) copy-start(f32[2,8,768]{2,1,0:T(8,128)} %param.36) | copy-start | bytes 147460
  531.7 6.3 %copy-start.31 = (f32[2,768,8]{1,2,0:T(8,128)S(1)}, f32[2,768,8]{1,2,0:T(8,128)}, u32[]{:S(2)}) copy-start(f32[2,768,8]{1,2,0:T(8,128)} %param.37) | copy-start | bytes 147460
  531.7 6.3 %copy-start.32 = (f32[2,768,8]{1,2,0:T(8,128)S(1)}, f32[2,768,8]{1,2,0:T(8,128)}, u32[]{:S(2)}) copy-start(f32[2,768,8]{1,2,0:T(8,128)} %param.35) | copy-start | bytes 147460
  (24 other events, 65.8 us)
Sparse Core Ops, SparseCore 0:
  10.9 62.8 all-gather.4
  76.7 52.9 all-gather.6
  132.7 62.4 all-gather.8
  197.9 61.8 all-gather.10
